TPU v7x, 256 devices: a whole 4x4x8 slice. The times are simulated.
256 devices in a mesh: dp: 32 (over z, y), mp: 8 (over x, core).
Axes of the slice: x: 4, y: 4, z: 8, core: 2. Of those that a mesh axis runs over, the one named last changes fastest.
Arguments:
- tokens: bfloat16 [8192, 4096], P('dp', 'mp'), may hold values from -24 to 24
- cotangent: bfloat16 [8192, 4096], P('dp', 'mp'), may hold values from -6 to 6
- gain_dec: float32 [4096], replicated, may hold values from 0.1 to 1.9
- w_query: bfloat16 [4096, 4096], P(None, 'mp'), may hold values from -1 to 1
- w_out: bfloat16 [4096, 4096], P('mp'), may hold values from -0.5 to 0.5
- encodings: bfloat16 [256, 128, 896], P('dp', 'mp'), may hold values from -24 to 24
- gain_enc: float32 [896], replicated, may hold values from 0.1 to 1.9
- w_key: bfloat16 [896, 4096], P(None, 'mp'), may hold values from -1 to 1
- w_value: bfloat16 [896, 4096], P(None, 'mp'), may hold values from -0.1875 to 0.1875
- gain_post: float32 [4096], replicated, may hold values from 0.1 to 1.9
- neighbour_ids: int32 [128, 2], P('dp'), may hold values from 0 to 255, as said below
Outputs:
- mixed: bfloat16 [8192, 4096], P('dp', 'mp')
- ffn_input: bfloat16 [8192, 4096], P('dp', 'mp')
- d_encodings: bfloat16 [256, 128, 896], P('dp', 'mp')
Inputs may be any that keep to these rules, and one draw needn't show every extreme that they name: `neighbour_ids`: encoder row g is held by index g // 8 of dp. Every encoder row is retrieved by exactly one block. The blocks of one index of dp retrieve at most 1 row held by any one index of dp, and exactly 1 from some.
All inputs are finite; a program needn't handle non-finite values.
Results may differ from a plain program's by a relative error of at most 0.02.
The roundings to bfloat16 on the way count: a program that leaves them out, or rounds other values in their place, can miss the bound.
Values may be sent and summed in bfloat16 or wider, within the bound.
No kernel may reach another device: no remote copies, remote signals or barrier semaphores. Data moves between devices by JAX's collectives and lax.ppermute only.
A program may use at most 64 MiB of HBM per device.

v0:
```python
import jax
import jax.numpy as jnp
from jax import lax
from jax.sharding import PartitionSpec as P

HD = 128
BLOCK = 64
NLEN = 128
NEIGH = 2


EPS = 1e-06


def rms_scale(values):
    return lax.rsqrt(jnp.mean(values * values, axis=-1, keepdims=True) + EPS)


def shards(
    tokens,
    cotangent,
    gain_dec,
    w_query,
    w_out,
    encodings,
    gain_enc,
    w_key,
    w_value,
    gain_post,
    neighbour_ids,
):
    dp_count = lax.axis_size("dp")
    seq_len = tokens.shape[0]
    share_cols = tokens.shape[1]
    head_cols = w_query.shape[1]
    heads_here = head_cols // HD
    own_rows = encodings.shape[0]
    blocks = neighbour_ids.shape[0]
    readings = blocks * neighbour_ids.shape[1]
    per_holder = (readings + dp_count - 1) // dp_count
    slot_count = dp_count * per_holder
    lead_in = BLOCK - 1
    score_scale = HD ** (-0.5)
    whole_x, whole_dy = (
        lax.all_gather(tokens, "mp", axis=1, tiled=True),
        lax.all_gather(cotangent, "mp", axis=1, tiled=True),
    )
    tok_wide = whole_x.astype(jnp.float32)
    normed = (tok_wide * rms_scale(tok_wide) * gain_dec).astype(jnp.bfloat16)
    queries = jnp.dot(normed, w_query, preferred_element_type=jnp.float32).astype(jnp.bfloat16)
    chosen = neighbour_ids.reshape(readings)
    owner_of = chosen // own_rows
    local_row = chosen % own_rows
    positions = jnp.arange(readings, dtype=jnp.int32)
    same_owner = owner_of[:, None] == owner_of[None, :]
    earlier = (chosen[None, :] < chosen[:, None]) | (chosen[None, :] == chosen[:, None]) & (
        positions[None, :] < positions[:, None]
    )
    slot_rank = jnp.sum((same_owner & earlier).astype(jnp.int32), axis=1)
    slot_of = owner_of * per_holder + slot_rank
    slot_ids = jnp.arange(slot_count, dtype=jnp.int32)
    matches = slot_of[:, None] == slot_ids[None, :]
    wanted = jnp.sum(jnp.where(matches, local_row[:, None] + 1, 0), axis=0) - 1
    requested = lax.all_to_all(
        wanted.reshape(dp_count, per_holder), "dp", split_axis=0, concat_axis=0, tiled=True
    ).reshape(slot_count)
    enc_wide = encodings.astype(jnp.float32)
    row_scale = rms_scale(enc_wide)
    normed_enc = (enc_wide * row_scale * gain_enc).astype(jnp.bfloat16)
    select = requested[:, None] == jnp.arange(own_rows, dtype=jnp.int32)[None, :]
    outgoing = jnp.einsum(
        "sj,jte->ste", select.astype(jnp.bfloat16), normed_enc, preferred_element_type=jnp.float32
    ).astype(jnp.bfloat16)
    incoming = lax.all_to_all(outgoing, "dp", split_axis=0, concat_axis=0, tiled=True)
    picked = jnp.einsum(
        "as,ste->ate", matches.astype(jnp.bfloat16), incoming, preferred_element_type=jnp.float32
    ).astype(jnp.bfloat16)
    w_both = jnp.concatenate([w_key, w_value], axis=1)
    key_values = jnp.einsum(
        "ate,ej->atj",
        lax.all_gather(picked, "mp", axis=1, tiled=True),
        w_both,
        preferred_element_type=jnp.float32,
    ).astype(jnp.bfloat16)
    key_blocks = key_values[..., :head_cols].reshape(blocks, NEIGH * NLEN, heads_here, HD)
    value_blocks = key_values[..., head_cols:].reshape(blocks, NEIGH * NLEN, heads_here, HD)
    pad_rows = jnp.zeros((lead_in, head_cols), jnp.bfloat16)
    shifted = jnp.concatenate([queries[lead_in:], pad_rows], axis=0).reshape(
        blocks, BLOCK, heads_here, HD
    )
    scores = (
        jnp.einsum("cqhd,ckhd->chqk", shifted, key_blocks, preferred_element_type=jnp.float32)
        * score_scale
    )
    row_max = jnp.max(scores, axis=-1, keepdims=True)
    lifted = jnp.exp(scores - row_max)
    probability = lifted / jnp.sum(lifted, axis=-1, keepdims=True)
    weights = probability.astype(jnp.bfloat16)
    attended = jnp.einsum(
        "chqk,ckhd->cqhd", weights, value_blocks, preferred_element_type=jnp.float32
    ).astype(jnp.bfloat16)
    attended = jnp.concatenate(
        [pad_rows, attended.reshape(seq_len, head_cols)[: seq_len - lead_in]], axis=0
    )
    branch = jnp.dot(attended, w_out, preferred_element_type=jnp.float32)
    column0 = lax.axis_index("mp") * share_cols
    summed = lax.psum(branch.astype(jnp.bfloat16), "mp").astype(jnp.float32)
    mixed_full = (tok_wide + summed).astype(jnp.bfloat16)
    mixed_wide = mixed_full.astype(jnp.float32)
    ffn_full = (mixed_wide * rms_scale(mixed_wide) * gain_post).astype(jnp.bfloat16)
    mixed_out = lax.dynamic_slice_in_dim(mixed_full, column0, share_cols, 1)
    ffn_out = lax.dynamic_slice_in_dim(ffn_full, column0, share_cols, 1)
    d_attended = lax.dot_general(
        whole_dy, w_out, (((1,), (1,)), ((), ())), preferred_element_type=jnp.float32
    ).astype(jnp.bfloat16)
    d_shifted = jnp.concatenate([d_attended[lead_in:], pad_rows], axis=0).reshape(
        blocks, BLOCK, heads_here, HD
    )
    value_grad = jnp.einsum(
        "chqk,cqhd->ckhd", weights, d_shifted, preferred_element_type=jnp.float32
    ).astype(jnp.bfloat16)
    d_probability = jnp.einsum(
        "cqhd,ckhd->chqk", d_shifted, value_blocks, preferred_element_type=jnp.float32
    )
    d_scores = (
        probability
        * (d_probability - jnp.sum(probability * d_probability, axis=-1, keepdims=True))
        * score_scale
    ).astype(jnp.bfloat16)
    key_grad = jnp.einsum(
        "chqk,cqhd->ckhd", d_scores, shifted, preferred_element_type=jnp.float32
    ).astype(jnp.bfloat16)
    both_grads = jnp.concatenate(
        [
            key_grad.reshape(readings, NLEN, head_cols),
            value_grad.reshape(readings, NLEN, head_cols),
        ],
        axis=2,
    )
    d_normed = lax.psum_scatter(
        jnp.einsum("atj,ej->tae", both_grads, w_both, preferred_element_type=jnp.float32).astype(
            jnp.bfloat16
        ),
        "mp",
        scatter_dimension=0,
        tiled=True,
    ).astype(jnp.float32)
    back_out = jnp.einsum(
        "as,tae->ste", matches.astype(jnp.float32), d_normed, precision=lax.Precision.HIGHEST
    )
    back_in = lax.all_to_all(back_out, "dp", split_axis=0, concat_axis=0, tiled=True)
    grad_rows = jnp.einsum(
        "sj,ste->jte", select.astype(jnp.float32), back_in, precision=lax.Precision.HIGHEST
    )
    enc_hat = enc_wide * row_scale
    upstream = gain_enc * grad_rows
    d_encodings = (
        row_scale * (upstream - enc_hat * jnp.mean(upstream * enc_hat, axis=-1, keepdims=True))
    ).astype(jnp.bfloat16)
    return (mixed_out, ffn_out, d_encodings)


def solution(mesh):
    in_specs = (
        P("dp", "mp"),
        P("dp", "mp"),
        P(),
        P(None, "mp"),
        P("mp", None),
        P("dp", "mp", None),
        P(),
        P(None, "mp"),
        P(None, "mp"),
        P(),
        P("dp", None),
    )
    out_specs = (P("dp", "mp"), P("dp", "mp"), P("dp", "mp", None))
    return jax.shard_map(shards, mesh=mesh, in_specs=in_specs, out_specs=out_specs, check_vma=False)
```

profile of v0, /device:TPU:8, one launch (start us, length us, event | category | flops | bytes accessed | tf_op | source)
XLA Modules:
  0.0 289.5 jit_solution(13301968982519094637)
XLA Ops:
  7.2 0.0 all-gather.8.cloned.1.call-start
  7.2 0.7 all-gather.8.cloned.1.call-update
  7.9 0.0 all-gather.4.cloned.1.call-start
  7.9 0.7 all-gather.4.cloned.1.call-update
  8.6 0.8 copy.93
  9.4 0.1 reshape.171
  9.5 0.2 convert_reduce_fusion
  9.7 0.1 select_reduce_fusion
  9.8 0.7 copy.94
  10.5 11.7 %all-to-all-start = ((s32[32,1,1]{2,1,0:T(1,128)}), s32[32,1,1]{2,1,0:T(1,128)S(1)}, u32[]{:S(2)}, u32[]{:S(2)}) async-start(s32[32,1,1]{2,1,0:T(1,128)} %copy.94), calls=%async_computation | async-start | bytes 32768 | tf_op jit(solution)/shard_map/all_to_all | solution.py:64
  22.2 0.0 all-gather.6.cloned.1.call-start
  22.3 1.1 fusion.49
  23.3 7.3 %all-to-all-done = s32[32,1,1]{2,1,0:T(1,128)S(1)} async-done(((s32[32,1,1]{2,1,0:T(1,128)}), s32[32,1,1]{2,1,0:T(1,128)S(1)}, u32[]{:S(2)}, u32[]{:S(2)}) %all-to-all-start) | async-done | bytes 160 | tf_op jit(solution)/shard_map/all_to_all | solution.py:64
  30.7 0.7 reduce
  31.3 1.4 convolution_convert_fusion.4
  32.7 0.3 copy.96
  33.0 28.3 %all_to_all.16 = bf16[32,16,896]{2,1,0:T(8,128)(2,1)S(1)} all-to-all(bf16[32,16,896]{2,1,0:T(8,128)(2,1)S(1)} %copy.96), channel_id=1, replica_groups=mesh['dp'=32,'mp'=8] {'dp'}, dimensions={0} | all-to-all | bytes 1835008 | tf_op jit(solution)/shard_map/all_to_all | solution.py:74
  61.3 1.0 convolution_convert_fusion.6
  62.3 0.0 all-gather.6.cloned.1.call-update
  62.3 0.0 reduce-scatter.2.cloned.1.call-start
  62.4 0.0 all-gather.8.cloned.1.call-done
  62.4 4.2 %fusion.84 = bf16[256,512]{1,0:T(8,128)(2,1)S(1)} fusion(bf16[256,4096]{1,0:T(8,128)(2,1)} %all-gather.8.cloned.1.call-done, bf16[512,4096]{1,0:T(8,128)(2,1)} %param.15), kind=kOutput, calls=%fused_computation.110 | convolution fusion | flops 1073741824 | bytes 6553600 | tf_op jit(solution)/shard_map/dot_general | solution.py:113
  66.6 0.1 slice.27
  66.7 0.1 reshape.176
  66.8 3.5 %all-gather.4.cloned.1.call-done = bf16[256,4096]{1,0:T(8,128)(2,1)} async-done(((bf16[256,512]{1,0:T(8,128)(2,1)}), bf16[256,4096]{1,0:T(8,128)(2,1)}) %all-gather.4.cloned.1.call-update) | async-done | bytes 2097168 | tf_op jit(solution)/shard_map/all_gather | solution.py:45
  70.3 2.2 fusion.2
  72.6 3.5 %fusion.6 = bf16[256,512]{1,0:T(8,128)(2,1)S(1)} fusion(bf16[4096,512]{1,0:T(8,128)(2,1)} %param.14, bf16[256,4096]{1,0:T(8,128)(2,1)S(1)} %copy-done, f32[4096]{0:T(1024)S(1)} %copy-done.4, f32[256]{0:T(256)S(1)} %add_rsqrt_fusion.2), kind=kOutput, calls=%fused_computation.11 | convolution fusion | flops 1077936128 | bytes 6571008 | tf_op jit(solution)/shard_map/dot_general | solution.py:50
  76.1 0.1 slice.28
  76.2 0.8 reshape.173
  76.9 23.5 %all-gather.6.cloned.1.call-done = bf16[8,128,896]{2,0,1:T(8,128)(2,1)} async-done(((bf16[8,16,896]{2,0,1:T(8,128)(2,1)}), bf16[8,128,896]{2,0,1:T(8,128)(2,1)}) %all-gather.6.cloned.1.call-update) | async-done | bytes 1835024 | tf_op jit(solution)/shard_map/all_gather | solution.py:81
  100.4 4.3 %convolution_convert_fusion.1 = bf16[8,128,1024]{2,1,0:T(8,128)(2,1)S(1)} fusion(bf16[8,128,896]{2,0,1:T(8,128)(2,1)} %all-gather.6.cloned.1.call-done, bf16[896,512]{1,0:T(8,128)(2,1)} %param.19, bf16[896,512]{1,0:T(8,128)(2,1)} %param.18), kind=kOutput, calls=%fused_computation.18 | convolution fusion | flops 1883766784 | bytes 5767168 | tf_op jit(solution)/shard_map/ate,ej->atj/dot_general | solution.py:79
  104.7 1.2 fusion.82
  105.9 1.2 reshape.174
  107.1 1.3 reshape.172
  108.4 1.8 convolution_multiply_fusion
  110.2 1.4 fusion.83
  111.7 1.5 fusion.34
  113.1 4.8 %fusion.21 = bf16[4,256,4,128]{1,3,2,0:T(8,128)(2,1)} fusion(bf16[4,64,4,128]{3,2,1,0:T(4,128)(2,1)S(1)} %reshape.176, f32[4,4,64]{2,1,0:T(4,128)S(1)} %get-tuple-element.27, f32[4,4,64,256]{3,2,1,0:T(8,128)} %copy-done.1), kind=kOutput, calls=%fused_computation.29 | convolution fusion | flops 68420864 | bytes 2363392 | tf_op jit(solution)/shard_map/chqk,cqhd->ckhd/dot_general | solution.py:119
  117.9 9.0 %fusion.20 = bf16[4,256,4,128]{1,3,2,0:T(8,128)(2,1)} fusion(f32[4,4,64,256]{3,2,1,0:T(8,128)} %fusion.34, bf16[4,64,4,128]{3,2,1,0:T(4,128)(2,1)} %reshape.173, f32[4,4,64,256]{3,2,1,0:T(8,128)} %get-tuple-element.28, f32[4,4,64]{2,1,0:T(4,128)S(1)} %get-tuple-element.27), kind=kOutput, calls=%fused_computation.28 | convolution fusion | flops 69469440 | bytes 3411968 | tf_op jit(solution)/shard_map/chqk,cqhd->ckhd/dot_general | solution.py:130
  126.9 2.4 copy.106
  129.3 2.3 reshape.177
  131.5 2.3 copy.108
  133.9 2.3 reshape.178
  136.1 5.4 %convert_bitcast_fusion = bf16[128,8,896]{0,2,1:T(8,128)(2,1)} fusion(bf16[8,128,512]{2,1,0:T(8,128)(2,1)} %reshape.178, bf16[8,128,512]{2,1,0:T(8,128)(2,1)} %reshape.177, bf16[896,512]{1,0:T(8,128)(2,1)} %param.19, bf16[896,512]{1,0:T(8,128)(2,1)} %param.18), kind=kOutput, calls=%fused_computation.23 | convolution fusion | flops 1887830016 | bytes 5767168 | tf_op jit(solution)/shard_map/atj,ej->tae/dot_general | solution.py:141
  141.6 3.9 %copy.109 = bf16[128,8,896]{2,1,0:T(8,128)(2,1)} copy(bf16[128,8,896]{0,2,1:T(8,128)(2,1)} %convert_bitcast_fusion) | data formatting | bytes 3670016 | tf_op jit(solution)/shard_map/convert_element_type | solution.py:141
  145.5 0.0 reduce-scatter.2.cloned.1.call-update
  145.5 36.1 %reduce-scatter.2.cloned.1.call-done = bf16[16,8,896]{2,1,0:T(8,128)(2,1)} async-done(((bf16[128,8,896]{2,1,0:T(8,128)(2,1)}), bf16[16,8,896]{2,1,0:T(8,128)(2,1)}) %reduce-scatter.2.cloned.1.call-update) | async-done | bytes 229392 | tf_op jit(solution)/shard_map/reduce_scatter | solution.py:140
  181.6 1.4 fusion.62
  183.1 2.3 copy.110
  185.4 10.2 %all-to-all-start.2 = ((f32[32,16,896]{2,1,0:T(8,128)}), f32[32,16,896]{2,1,0:T(8,128)}, u32[]{:S(2)}, u32[]{:S(2)}) async-start(f32[32,16,896]{2,1,0:T(8,128)} %copy.110), calls=%async_computation.3 | async-start | bytes 3670016 | tf_op jit(solution)/shard_map/all_to_all | solution.py:151
  195.6 0.3 all-reduce.5.cloned.1.call-start
  195.9 3.5 %fusion.30 = bf16[4,64,4,128]{3,1,2,0:T(8,128)(2,1)S(1)} fusion(bf16[4,256,4,128]{3,2,1,0:T(4,128)(2,1)S(1)} %reshape.172, f32[4,4,64]{2,1,0:T(4,128)S(1)} %get-tuple-element.27, f32[4,4,64,256]{3,2,1,0:T(8,128)} %copy-done.1), kind=kOutput, calls=%fused_computation.39 | convolution fusion | flops 68027648 | bytes 2363392 | tf_op jit(solution)/shard_map/chqk,ckhd->cqhd/dot_general | solution.py:99
  199.4 0.2 copy.102
  199.7 4.7 %convolution_convert_fusion = bf16[256,4096]{1,0:T(8,128)(2,1)} fusion(bf16[512,4096]{1,0:T(8,128)(2,1)} %param.15, bf16[193,512]{1,0:T(8,128)(2,1)S(1)} %slice.23), kind=kOutput, calls=%fused_computation.5 | convolution fusion | flops 1074790400 | bytes 6489088 | tf_op jit(solution)/shard_map/dot_general | solution.py:105
  204.5 0.0 all-reduce.5.cloned.1.call-update
  204.5 0.8 dynamic-slice
  205.2 69.5 %all-reduce.5.cloned.1.call-done = bf16[256,4096]{1,0:T(8,128)(2,1)} async-done(((bf16[256,4096]{1,0:T(8,128)(2,1)}), bf16[256,4096]{1,0:T(8,128)(2,1)}) %all-reduce.5.cloned.1.call-update) | async-done | bytes 2097168 | tf_op jit(solution)/shard_map/psum | solution.py:107
  274.7 2.5 multiply_reduce_fusion
  277.3 0.5 convert_element_type.98
  277.8 0.7 constant_dynamic-slice_fusion
  278.5 0.8 fusion.42
  279.3 2.8 fusion.45
  282.1 0.2 fusion.48
  282.3 0.7 copy.112
  (22 shorter events, 0.2 us)
Async XLA Ops:
  7.2 55.3 %all-gather.8.cloned.1.call-start = ((), (), s32[]{:S(2)}) async-start(), calls=%async_computation.7 | async-start | bytes 2359296 | tf_op jit(solution)/shard_map/all_gather | solution.py:46
  7.9 62.4 %all-gather.4.cloned.1.call-start = ((), (), s32[]{:S(2)}) async-start(), calls=%async_computation.4 | async-start | bytes 2359296 | tf_op jit(solution)/shard_map/all_gather | solution.py:45
  10.5 20.2 %all-to-all-start = ((s32[32,1,1]{2,1,0:T(1,128)}), s32[32,1,1]{2,1,0:T(1,128)S(1)}, u32[]{:S(2)}, u32[]{:S(2)}) async-start(s32[32,1,1]{2,1,0:T(1,128)} %copy.94), calls=%async_computation | async-start | bytes 32768 | tf_op jit(solution)/shard_map/all_to_all | solution.py:64
  22.2 78.2 %all-gather.6.cloned.1.call-start = ((), (), s32[]{:S(2)}) async-start(), calls=%async_computation.5 | async-start | bytes 2064384 | tf_op jit(solution)/shard_map/all_gather | solution.py:81
  62.3 119.3 %reduce-scatter.2.cloned.1.call-start = ((), (), s32[]{:S(2)}) async-start(), calls=%async_computation.8 | async-start | bytes 2064384 | tf_op jit(solution)/shard_map/reduce_scatter | solution.py:140
  66.6 6.0 %copy-start.4 = (f32[4096]{0:T(1024)S(1)}, f32[4096]{0:T(1024)}, u32[]{:S(2)}) copy-start(f32[4096]{0:T(1024)} %param.13) | copy-start | bytes 49156
  70.3 2.3 copy-start
  110.2 2.9 copy-start.1
  185.4 93.9 %all-to-all-start.2 = ((f32[32,16,896]{2,1,0:T(8,128)}), f32[32,16,896]{2,1,0:T(8,128)}, u32[]{:S(2)}, u32[]{:S(2)}) async-start(f32[32,16,896]{2,1,0:T(8,128)} %copy.110), calls=%async_computation.3 | async-start | bytes 3670016 | tf_op jit(solution)/shard_map/all_to_all | solution.py:151
  195.6 79.1 %all-reduce.5.cloned.1.call-start = ((), (), s32[]{:S(2)}) async-start(), calls=%async_computation.6 | async-start | bytes 4194304 | tf_op jit(solution)/shard_map/psum | solution.py:107
  277.3 2.1 copy-start.2
  277.3 2.1 copy-start.3
Sparse Core Ops, SparseCore 0:
  9.8 30.5 all-gather.7
  42.3 28.0 all-gather.3
  72.8 27.5 all-gather.5
  145.7 35.9 reduce-scatter.1
  204.6 70.0 all-reduce.4
where the time goes:
time: 290 us
  waiting for transfers between devices  141 us (49%)
  matrix products  49.4 us (17%)
  blocking collectives  28.3 us (10%)
  local copies, waits for them, and re-layouts  24.5 us (8%)
  starting transfers between devices  22.3 us (8%)
  between operations  14 us (5%)
  other arithmetic  9.75 us (3%)
    psum x1, waiting for transfers between devices, shards(): summed = lax.psum(branch.astype(jnp.bfloat16), 'mp').astype(jnp.float32)  69.5 us
    reduce_scatter x1, waiting for transfers between devices, shards(): lax.psum_scatter(jnp.einsum('atj,ej->tae', both_grads, w_both, preferred_...  36.1 us
    all_to_all x1, blocking collectives, shards(): lax.all_to_all(outgoing, 'dp', split_axis=0, concat_axis=0, tiled=True)  28.3 us
    all_gather x1, waiting for transfers between devices, shards(): lax.all_gather(picked, 'mp', axis=1, tiled=True)  23.5 us
    all_to_all x1, starting transfers between devices, shards(): lax.all_to_all(wanted.reshape(dp_count, per_holder), 'dp', split_axis=0,...  11.7 us
    all_to_all x1, starting transfers between devices, shards(): lax.all_to_all(back_out, 'dp', split_axis=0, concat_axis=0, tiled=True)  10.2 us
    dot_general x1, matrix products, shards(): jnp.einsum('chqk,cqhd->ckhd', d_scores, shifted, preferred_element_type=j...  9.05 us
    all_to_all x1, waiting for transfers between devices, shards(): lax.all_to_all(wanted.reshape(dp_count, per_holder), 'dp', split_axis=0,...  7.32 us
  transfers between devices with their start and end apart: 7, of which 5 were waited for; matrix products, arithmetic and copies ran while one was open for 11% of the time, Pallas kernels for 0%

commit v1 on v0

v1 whole, which is shorter than its diff:
```python
import jax
import jax.numpy as jnp
from jax import lax
from jax.experimental import pallas as pl
from jax.experimental.pallas import tpu as pltpu
from jax.sharding import PartitionSpec as P

HD = 128
BLOCK = 64
NLEN = 128
NEIGH = 2

EPS = 1e-06
F32 = jnp.float32
BF16 = jnp.bfloat16
VMEM_LIMIT = 48 * 1024 * 1024


def rms_scale(values):
    return lax.rsqrt(jnp.mean(values * values, axis=-1, keepdims=True) + EPS)


def params():
    return pltpu.CompilerParams(vmem_limit_bytes=VMEM_LIMIT)


def vmem():
    return pl.BlockSpec(memory_space=pltpu.VMEM)


def hbm():
    return pl.BlockSpec(memory_space=pl.ANY)


def smem():
    return pl.BlockSpec(memory_space=pltpu.SMEM)


def chip_shift(count, k):
    return [(i, (i + 2 * k) % count) for i in range(count)]


def core_swap(count):
    return [(i, i ^ 1) for i in range(count)]


def gather_pieces(x, count):
    own = [x] + [lax.ppermute(x, "mp", chip_shift(count, k)) for k in range(1, count // 2)]
    return own + [lax.ppermute(p, "mp", core_swap(count)) for p in own]


def scatter_sum(send, keep, count):
    both = keep.astype(F32) + lax.ppermute(send, "mp", core_swap(count)).astype(F32)
    pair = both.astype(BF16)
    total = pair[0].astype(F32)
    for k in range(1, count // 2):
        total = total + lax.ppermute(pair[k], "mp", chip_shift(count, -k)).astype(F32)
    return total


def shift_matrix(n, lead, transpose):
    r = lax.broadcasted_iota(jnp.int32, (n, n), 0)
    c = lax.broadcasted_iota(jnp.int32, (n, n), 1)
    hit = (r == c + lead) if transpose else (c == r + lead)
    return jnp.where(hit, 1.0, 0.0).astype(BF16)


def dot(a, b):
    return lax.dot_general(a, b, (((1,), (0,)), ((), ())), preferred_element_type=F32)


def dot_nt(a, b):
    return lax.dot_general(a, b, (((1,), (1,)), ((), ())), preferred_element_type=F32)


def dot_tn(a, b):
    return lax.dot_general(a, b, (((0,), (0,)), ((), ())), preferred_element_type=F32)


def query_kernel(count, src, *refs):
    pieces = refs[:count]
    gain, w_hbm, out, w_buf, sems = refs[count:]
    share = pieces[0].shape[1]
    copies = []
    for k in range(count):
        start = pl.multiple_of(src[k] * share, share)
        cp = pltpu.make_async_copy(w_hbm.at[pl.ds(start, share), :], w_buf.at[k], sems.at[k])
        cp.start()
        copies.append(cp)
    squares = jnp.zeros((pieces[0].shape[0], 1), F32)
    for k in range(count):
        wide = pieces[k][...].astype(F32)
        squares = squares + jnp.sum(wide * wide, axis=1, keepdims=True)
    scale = lax.rsqrt(squares / (share * count) + EPS)
    acc = jnp.zeros(out.shape, F32)
    for k in range(count):
        g = gain[pl.ds(src[k], 1), :]
        normed = (pieces[k][...].astype(F32) * scale * g).astype(BF16)
        copies[k].wait()
        acc = acc + dot(normed, w_buf[k])
    out[...] = dot(shift_matrix(out.shape[0], BLOCK - 1, False), acc.astype(BF16)).astype(BF16)


def run_query(src, pieces, gain, w_query):
    count = len(pieces)
    rows, share = pieces[0].shape
    cols = w_query.shape[1]
    return pl.pallas_call(
        lambda *r: query_kernel(count, *r),
        out_shape=jax.ShapeDtypeStruct((rows, cols), BF16),
        in_specs=[smem()] + [vmem()] * count + [vmem(), hbm()],
        out_specs=vmem(),
        scratch_shapes=[pltpu.VMEM((count, share, cols), BF16), pltpu.SemaphoreType.DMA((count,))],
        compiler_params=params(),
        name="queries",
    )(src, *pieces, gain.reshape(count, share), w_query)


def back_kernel(count, src, *refs):
    pieces = refs[:count]
    w_hbm, out, w_buf, sems = refs[count:]
    share = pieces[0].shape[1]
    copies = []
    for k in range(count):
        start = pl.multiple_of(src[k] * share, share)
        cp = pltpu.make_async_copy(w_hbm.at[:, pl.ds(start, share)], w_buf.at[k], sems.at[k])
        cp.start()
        copies.append(cp)
    acc = jnp.zeros(out.shape, F32)
    for k in range(count):
        copies[k].wait()
        acc = acc + dot_nt(pieces[k][...], w_buf[k])
    out[...] = dot(shift_matrix(out.shape[0], BLOCK - 1, False), acc.astype(BF16)).astype(BF16)


def run_back(src, pieces, w_out):
    count = len(pieces)
    rows, share = pieces[0].shape
    cols = w_out.shape[0]
    return pl.pallas_call(
        lambda *r: back_kernel(count, *r),
        out_shape=jax.ShapeDtypeStruct((rows, cols), BF16),
        in_specs=[smem()] + [vmem()] * count + [hbm()],
        out_specs=vmem(),
        scratch_shapes=[pltpu.VMEM((count, cols, share), BF16), pltpu.SemaphoreType.DMA((count,))],
        compiler_params=params(),
        name="d_attended",
    )(src, *pieces, w_out)


def branch_kernel(count, src, att, w_hbm, send, keep, w_buf, sems):
    share = send.shape[2]
    half = count // 2
    copies = []
    order = list(range(half, count)) + list(range(half))
    for k in order:
        start = pl.multiple_of(src[k] * share, share)
        cp = pltpu.make_async_copy(w_hbm.at[:, pl.ds(start, share)], w_buf.at[k], sems.at[k])
        cp.start()
        copies.append(cp)
    a = att[...]
    for k, cp in zip(order, copies):
        cp.wait()
        part = dot(a, w_buf[k]).astype(BF16)
        if k < half:
            keep[k] = part
        else:
            send[k - half] = part


def run_branch(src, att, w_out, count):
    rows, cols = att.shape
    share = w_out.shape[1] // count
    shape = jax.ShapeDtypeStruct((count // 2, rows, share), BF16)
    return pl.pallas_call(
        lambda *r: branch_kernel(count, *r),
        out_shape=(shape, shape),
        in_specs=[smem(), vmem(), hbm()],
        out_specs=(vmem(), vmem()),
        scratch_shapes=[pltpu.VMEM((count, cols, share), BF16), pltpu.SemaphoreType.DMA((count,))],
        compiler_params=params(),
        name="branches",
    )(src, att, w_out)


def attention_kernel(count, blocks, *refs):
    pieces = refs[:count]
    q_ref, d_ref, wk, wv, send, keep, att_out, mem, keys, values, k_grad, v_grad, att = refs[count:]
    heads = q_ref.shape[1] // HD
    part = pieces[0].shape[0] // blocks
    span = part * count
    half = count // 2
    scale = HD ** (-0.5)
    for b in range(blocks):
        for k in range(count):
            mem[b * span + k * part : b * span + (k + 1) * part, :] = pieces[k][
                b * part : (b + 1) * part, :
            ]
    keys[...] = dot(mem[...], wk[...]).astype(BF16)
    values[...] = dot(mem[...], wv[...]).astype(BF16)
    for b in range(blocks):
        rows = slice(b * BLOCK, (b + 1) * BLOCK)
        ctx = slice(b * span, (b + 1) * span)
        for h in range(heads):
            cols = slice(h * HD, (h + 1) * HD)
            q = q_ref[rows, cols]
            d = d_ref[rows, cols]
            kk = keys[ctx, cols]
            vv = values[ctx, cols]
            scores = dot_nt(q, kk) * scale
            lifted = jnp.exp(scores - jnp.max(scores, axis=-1, keepdims=True))
            prob = lifted / jnp.sum(lifted, axis=-1, keepdims=True)
            weights = prob.astype(BF16)
            att[rows, cols] = dot(weights, vv).astype(BF16)
            d_prob = dot_nt(d, vv)
            d_scores = (
                prob * (d_prob - jnp.sum(prob * d_prob, axis=-1, keepdims=True)) * scale
            ).astype(BF16)
            v_grad[ctx, cols] = dot_tn(weights, d).astype(BF16)
            k_grad[ctx, cols] = dot_tn(d_scores, q).astype(BF16)
    att_out[...] = dot(shift_matrix(att.shape[0], BLOCK - 1, True), att[...]).astype(BF16)
    for b in range(blocks):
        ctx = slice(b * span, (b + 1) * span)
        terms = (dot_nt(k_grad[ctx, :], wk[...]) + dot_nt(v_grad[ctx, :], wv[...])).astype(BF16)
        for k in range(count):
            rows = terms[k * part : (k + 1) * part, :]
            if k < half:
                keep[k, b * part : (b + 1) * part, :] = rows
            else:
                send[k - half, b * part : (b + 1) * part, :] = rows


def run_attention(pieces, q, d, w_key, w_value, blocks):
    count = len(pieces)
    rows, width = pieces[0].shape
    cols = q.shape[1]
    shape = jax.ShapeDtypeStruct((count // 2, rows, width), BF16)
    total = rows * count
    return pl.pallas_call(
        lambda *r: attention_kernel(count, blocks, *r),
        out_shape=(shape, shape, jax.ShapeDtypeStruct(q.shape, BF16)),
        in_specs=[vmem()] * (count + 4),
        out_specs=(vmem(), vmem(), vmem()),
        scratch_shapes=[pltpu.VMEM((total, width), BF16)]
        + [pltpu.VMEM((total, cols), BF16)] * 4
        + [pltpu.VMEM(q.shape, BF16)],
        compiler_params=params(),
        name="attention",
    )(*pieces, q, d, w_key, w_value)


def outgoing_kernel(req, enc, gain, out, normed):
    wide = enc[...].astype(F32)
    normed[...] = (wide * rms_scale(wide) * gain[...]).astype(BF16)
    for s in range(out.shape[0]):
        out[s] = normed[jnp.maximum(req[s], 0)]


def run_outgoing(requested, encodings, gain):
    slots = requested.shape[0]
    return pl.pallas_call(
        outgoing_kernel,
        out_shape=jax.ShapeDtypeStruct((slots,) + encodings.shape[1:], BF16),
        in_specs=[smem(), vmem(), vmem()],
        out_specs=vmem(),
        scratch_shapes=[pltpu.VMEM(encodings.shape, BF16)],
        compiler_params=params(),
        name="outgoing_rows",
    )(requested, encodings, gain.reshape(1, 1, -1))


def pick_kernel(owner, rows, out, sems):
    copies = []
    for a in range(out.shape[0]):
        cp = pltpu.make_async_copy(rows.at[owner[a]], out.at[a], sems.at[a])
        cp.start()
        copies.append(cp)
    for cp in copies:
        cp.wait()


def run_pick(owner, rows):
    n = owner.shape[0]
    return pl.pallas_call(
        pick_kernel,
        out_shape=jax.ShapeDtypeStruct((n,) + rows.shape[1:], rows.dtype),
        in_specs=[smem(), hbm()],
        out_specs=vmem(),
        scratch_shapes=[pltpu.SemaphoreType.DMA((n,))],
        compiler_params=params(),
        name="picked_rows",
    )(owner, rows)


def place_kernel(reading, own, r1, r2, r3, out, total):
    total[...] = (
        own[...].astype(F32) + r1[...].astype(F32) + r2[...].astype(F32) + r3[...].astype(F32)
    ).astype(BF16)
    for s in range(out.shape[0]):
        out[s] = total[reading[s]]


def run_place(reading, parts):
    slots = reading.shape[0]
    shape = parts[0].shape
    return pl.pallas_call(
        place_kernel,
        out_shape=jax.ShapeDtypeStruct((slots,) + shape[1:], BF16),
        in_specs=[smem()] + [vmem()] * 4,
        out_specs=vmem(),
        scratch_shapes=[pltpu.VMEM(shape, BF16)],
        compiler_params=params(),
        name="placed_grads",
    )(reading, *parts)


def finish_kernel(slot, back, enc, gain, out, buf, sems):
    copies = []
    for j in range(out.shape[0]):
        cp = pltpu.make_async_copy(back.at[slot[j]], buf.at[j], sems.at[j])
        cp.start()
        copies.append(cp)
    wide = enc[...].astype(F32)
    scale = rms_scale(wide)
    hat = wide * scale
    for cp in copies:
        cp.wait()
    up = gain[...] * buf[...].astype(F32)
    out[...] = (scale * (up - hat * jnp.mean(up * hat, axis=-1, keepdims=True))).astype(BF16)


def run_finish(slot, back, encodings, gain):
    rows = encodings.shape[0]
    return pl.pallas_call(
        finish_kernel,
        out_shape=jax.ShapeDtypeStruct(encodings.shape, BF16),
        in_specs=[smem(), hbm(), vmem(), vmem()],
        out_specs=vmem(),
        scratch_shapes=[pltpu.VMEM(encodings.shape, BF16), pltpu.SemaphoreType.DMA((rows,))],
        compiler_params=params(),
        name="d_encodings",
    )(slot, back, encodings, gain.reshape(1, 1, -1))


def shards(
    tokens,
    cotangent,
    gain_dec,
    w_query,
    w_out,
    encodings,
    gain_enc,
    w_key,
    w_value,
    gain_post,
    neighbour_ids,
):
    dp_count = lax.axis_size("dp")
    count = lax.axis_size("mp")
    half = count // 2
    share_cols = tokens.shape[1]
    own_rows, own_tokens, width = encodings.shape
    blocks = neighbour_ids.shape[0]
    readings = blocks * neighbour_ids.shape[1]
    here = lax.axis_index("mp")
    steps = jnp.arange(half, dtype=jnp.int32)
    same = (here - 2 * steps) % count
    src = jnp.concatenate([same, same ^ 1]).astype(jnp.int32)

    chosen = neighbour_ids.reshape(readings)
    owner = chosen // own_rows
    local_row = chosen % own_rows
    slots = jnp.arange(dp_count, dtype=jnp.int32)
    matches = owner[:, None] == slots[None, :]
    wanted = jnp.sum(jnp.where(matches, local_row[:, None] + 1, 0), axis=0) - 1
    reading = jnp.sum(
        jnp.where(matches, jnp.arange(readings, dtype=jnp.int32)[:, None], 0), axis=0
    )
    requested = lax.all_to_all(
        wanted.reshape(dp_count, 1), "dp", split_axis=0, concat_axis=0, tiled=True
    ).reshape(dp_count)
    serves = requested[:, None] == jnp.arange(own_rows, dtype=jnp.int32)[None, :]
    slot = jnp.sum(jnp.where(serves, slots[:, None], 0), axis=0)

    tok_pieces = gather_pieces(tokens, count)
    cot_pieces = gather_pieces(cotangent, count)
    outgoing = run_outgoing(requested, encodings, gain_enc)
    incoming = lax.all_to_all(outgoing, "dp", split_axis=0, concat_axis=0, tiled=True)
    picked = run_pick(owner, incoming)
    row_pieces = gather_pieces(picked.reshape(readings * own_tokens, width), count)
    q = run_query(src, tok_pieces, gain_dec, w_query)
    d = run_back(src, cot_pieces, w_out)
    send, keep, attended = run_attention(row_pieces, q, d, w_key, w_value, blocks)

    swapped = lax.ppermute(send, "mp", core_swap(count))
    pair = (keep.astype(F32) + swapped.astype(F32)).astype(BF16)
    parts = [pair[0]] + [
        lax.ppermute(pair[k], "mp", chip_shift(count, -k)) for k in range(1, half)
    ]
    back_out = run_place(
        reading, [p.reshape(readings, own_tokens, width) for p in parts]
    )
    back_in = lax.all_to_all(back_out, "dp", split_axis=0, concat_axis=0, tiled=True)

    b_send, b_keep = run_branch(src, attended, w_out, count)
    summed = scatter_sum(b_send, b_keep, count)
    mixed = (tokens.astype(F32) + summed).astype(BF16)
    mixed_wide = mixed.astype(F32)
    squares = jnp.sum(mixed_wide * mixed_wide, axis=1)
    squares = squares + lax.ppermute(squares, "mp", core_swap(count))
    total = squares
    for k in range(1, half):
        total = total + lax.ppermute(squares, "mp", chip_shift(count, k))
    post = lax.rsqrt(total / (share_cols * count) + EPS)[:, None]
    gain_here = lax.dynamic_slice_in_dim(gain_post, here * share_cols, share_cols, 0)
    ffn = (mixed_wide * post * gain_here).astype(BF16)

    d_encodings = run_finish(slot, back_in, encodings, gain_enc)
    return (mixed, ffn, d_encodings)


def solution(mesh):
    in_specs = (
        P("dp", "mp"),
        P("dp", "mp"),
        P(),
        P(None, "mp"),
        P("mp", None),
        P("dp", "mp", None),
        P(),
        P(None, "mp"),
        P(None, "mp"),
        P(),
        P("dp", None),
    )
    out_specs = (P("dp", "mp"), P("dp", "mp"), P("dp", "mp", None))
    return jax.shard_map(shards, mesh=mesh, in_specs=in_specs, out_specs=out_specs, check_vma=False)
```

time: 290 us -> 158 us (0.54)
  waiting for transfers between devices: 141 us -> 55.3 us
  matrix products: 49.4 us -> 0 us
  starting transfers between devices: 22.3 us -> 58.6 us
  Pallas kernels: 0 us -> 32 us
  blocking collectives: 28.3 us -> 0 us
  local copies, waits for them, and re-layouts: 24.5 us -> 5.8 us
  between operations: 14 us -> 1.08 us
  other arithmetic: 9.75 us -> 3.83 us
    psum x1 -> x0, waiting for transfers between devices: 69.5 us -> none  [shards(): summed = lax.psum(branch.astype(jnp.bfloat16), 'mp').astype(jnp.float32)]
    dot_general x14 -> x0, matrix products: 49.4 us -> none  [the longest x1 9.05 us: shards(): jnp.einsum('chqk,cqhd->ckhd', d_scores, shifted, preferred_element_type=j...]
    ppermute x0 -> x33, waiting for transfers between devices: none -> 47.5 us  [the longest x9 22.6 us: gather_pieces(): lax.ppermute(x, 'mp', chip_shift(count, k))]
    reduce_scatter x1 -> x0, waiting for transfers between devices: 36.1 us -> none  [shards(): lax.psum_scatter(jnp.einsum('atj,ej->tae', both_grads, w_both, preferred_...]
    ppermute x0 -> x33, starting transfers between devices: none -> 32 us  [the longest x9 16.7 us: gather_pieces(): lax.ppermute(x, 'mp', chip_shift(count, k))]
    pallas_call x0 -> x8, Pallas kernels: none -> 32 us  [the longest x1 12.7 us: run_attention(): pl.pallas_call(lambda *r: attention_kernel(count, blocks, *r), out_shape=...]
    all_to_all x1 -> x0, blocking collectives: 28.3 us -> none  [shards(): lax.all_to_all(outgoing, 'dp', split_axis=0, concat_axis=0, tiled=True)]
    all_gather x3 -> x0, waiting for transfers between devices: 27 us -> none  [the longest x1 23.5 us: shards(): lax.all_gather(picked, 'mp', axis=1, tiled=True)]
  transfers between devices with their start and end apart: 7 -> 36, of which waited for: 5 -> 17; matrix products, arithmetic and copies ran while one was open for 11% -> 3% of each run, Pallas kernels for 0% -> 10%
where the time goes in v1:
time: 158 us; the launch traced here: 157 us
  starting transfers between devices  58.6 us (37%)
  waiting for transfers between devices  55.3 us (35%)
  Pallas kernels  32 us (20%)
  local copies, waits for them, and re-layouts  5.8 us (4%)
  other arithmetic  3.83 us (2%)
    ppermute x9, waiting for transfers between devices, gather_pieces(): lax.ppermute(x, 'mp', chip_shift(count, k))  22.6 us
    ppermute x9, starting transfers between devices, gather_pieces(): lax.ppermute(x, 'mp', chip_shift(count, k))  16.7 us
    ppermute x3, waiting for transfers between devices, scatter_sum(): lax.ppermute(pair[k], 'mp', chip_shift(count, -k)).astype(F32)  13.5 us
    pallas_call x1, Pallas kernels, run_attention(): pl.pallas_call(lambda *r: attention_kernel(count, blocks, *r), out_shape=...  12.7 us
    all_to_all x1, starting transfers between devices, shards(): lax.all_to_all(wanted.reshape(dp_count, 1), 'dp', split_axis=0, concat_ax...  11.7 us
    all_to_all x1, starting transfers between devices, shards(): lax.all_to_all(back_out, 'dp', split_axis=0, concat_axis=0, tiled=True)  9.9 us
    ppermute x3, waiting for transfers between devices, shards(): lax.ppermute(pair[k], 'mp', chip_shift(count, -k))  9.04 us
    all_to_all x1, waiting for transfers between devices, shards(): lax.all_to_all(wanted.reshape(dp_count, 1), 'dp', split_axis=0, concat_ax...  7.76 us
  transfers between devices with their start and end apart: 36, of which 17 were waited for; matrix products, arithmetic and copies ran while one was open for 3% of the time, Pallas kernels for 10%

profile of v1, /device:TPU:8, one launch (start us, length us, event | category | flops | bytes accessed | tf_op | source)
XLA Modules:
  0.0 156.6 jit_solution(3833961741070481371)
XLA Ops:
  0.6 0.8 copy.20
  1.4 0.1 reshape.101
  1.5 0.1 select_reduce_fusion
  1.6 0.7 copy.21
  2.3 11.7 %all-to-all-start = ((s32[32,1,1]{2,1,0:T(1,128)}), s32[32,1,1]{2,1,0:T(1,128)S(1)}, u32[]{:S(2)}, u32[]{:S(2)}) async-start(s32[32,1,1]{2,1,0:T(1,128)} %copy.21), calls=%async_computation | async-start | bytes 32768 | tf_op jit(solution)/shard_map/all_to_all | solution.py:379
  14.0 0.7 reshape.103.gain
  14.7 7.8 %all-to-all-done = s32[32,1,1]{2,1,0:T(1,128)S(1)} async-done(((s32[32,1,1]{2,1,0:T(1,128)}), s32[32,1,1]{2,1,0:T(1,128)S(1)}, u32[]{:S(2)}, u32[]{:S(2)}) %all-to-all-start) | async-done | bytes 160 | tf_op jit(solution)/shard_map/all_to_all | solution.py:379
  22.5 0.7 reduce.req
  23.2 0.9 copy-done.2
  24.1 1.7 %outgoing_rows.1 = bf16[32,16,896]{2,1,0:T(8,128)(2,1)} custom-call(s32[32]{0:T(128)S(1)} %reduce.req, bf16[8,16,896]{2,1,0:T(8,128)(2,1)S(1)} %copy-done.2, f32[1,1,896]{2,1,0:T(1,128)S(1)} %reshape.103.gain), custom_call_target="tpu_custom_call" | custom-call | tf_op jit(solution)/shard_map/outgoing_rows/pallas_call | solution.py:261
  25.8 5.0 %all-to-all-start.1 = ((bf16[32,16,896]{2,1,0:T(8,128)(2,1)}), bf16[32,16,896]{2,1,0:T(8,128)(2,1)S(1)}, u32[]{:S(2)}, u32[]{:S(2)}) async-start(bf16[32,16,896]{2,1,0:T(8,128)(2,1)} %outgoing_rows.1), calls=%async_computation.1 | async-start | bytes 1835008 | tf_op jit(solution)/shard_map/all_to_all | solution.py:388
  30.8 1.6 %collective-permute-start.7 = (bf16[256,512]{1,0:T(8,128)(2,1)S(1)}, bf16[256,512]{1,0:T(8,128)(2,1)S(1)}, u32[]{:S(2)}, u32[]{:S(2)}) collective-permute-start(bf16[256,512]{1,0:T(8,128)(2,1)S(1)} %copy-done), channel_id=1, source_target_pairs={{0,2},{1,3},{2,4},{3,5},{4,6},{5,7},{6,0},{7,1},{8,10},{9,11},{10,... | collective-permute-start | bytes 786440 | tf_op jit(solution)/shard_map/ppermute | solution.py:48
  32.4 2.7 %collective-permute-start.8 = (bf16[256,512]{1,0:T(8,128)(2,1)S(1)}, bf16[256,512]{1,0:T(8,128)(2,1)S(1)}, u32[]{:S(2)}, u32[]{:S(2)}) collective-permute-start(bf16[256,512]{1,0:T(8,128)(2,1)S(1)} %copy-done), channel_id=1, source_target_pairs={{0,4},{1,5},{2,6},{3,7},{4,0},{5,1},{6,2},{7,3},{8,12},{9,13},{10,... | collective-permute-start | bytes 786440 | tf_op jit(solution)/shard_map/ppermute | solution.py:48
  35.1 1.4 collective-permute-start.9
  36.6 0.6 collective-permute-start.14
  37.2 3.3 %collective-permute-done.7.r_2_ = bf16[256,512]{1,0:T(8,128)(2,1)S(1)} collective-permute-done((bf16[256,512]{1,0:T(8,128)(2,1)S(1)}, bf16[256,512]{1,0:T(8,128)(2,1)S(1)}, u32[]{:S(2)}, u32[]{:S(2)}) %collective-permute-start.7) | collective-permute-done | bytes 262176 | tf_op jit(solution)/shard_map/ppermute | solution.py:48
  40.5 5.0 %collective-permute-start.15 = (bf16[256,512]{1,0:T(8,128)(2,1)S(1)}, bf16[256,512]{1,0:T(8,128)(2,1)S(1)}, u32[]{:S(2)}, u32[]{:S(2)}) collective-permute-start(bf16[256,512]{1,0:T(8,128)(2,1)S(1)} %copy-done.4), channel_id=1, source_target_pairs={{0,4},{1,5},{2,6},{3,7},{4,0},{5,1},{6,2},{7,3},{8,12},{9,13},{10,... | collective-permute-start | bytes 786440 | tf_op jit(solution)/shard_map/ppermute | solution.py:48
  45.5 2.5 %collective-permute-done.8.r_3_ = bf16[256,512]{1,0:T(8,128)(2,1)S(1)} collective-permute-done((bf16[256,512]{1,0:T(8,128)(2,1)S(1)}, bf16[256,512]{1,0:T(8,128)(2,1)S(1)}, u32[]{:S(2)}, u32[]{:S(2)}) %collective-permute-start.8) | collective-permute-done | bytes 262176 | tf_op jit(solution)/shard_map/ppermute | solution.py:48
  48.0 0.6 collective-permute-done.9.r_4_
  48.6 0.5 collective-permute-start.11
  49.1 3.0 %collective-permute-done.14.r_2_ = bf16[256,512]{1,0:T(8,128)(2,1)S(1)} collective-permute-done((bf16[256,512]{1,0:T(8,128)(2,1)S(1)}, bf16[256,512]{1,0:T(8,128)(2,1)S(1)}, u32[]{:S(2)}, u32[]{:S(2)}) %collective-permute-start.14) | collective-permute-done | bytes 262176 | tf_op jit(solution)/shard_map/ppermute | solution.py:48
  52.1 4.2 %collective-permute-done.15.r_3_ = bf16[256,512]{1,0:T(8,128)(2,1)S(1)} collective-permute-done((bf16[256,512]{1,0:T(8,128)(2,1)S(1)}, bf16[256,512]{1,0:T(8,128)(2,1)S(1)}, u32[]{:S(2)}, u32[]{:S(2)}) %collective-permute-start.15) | collective-permute-done | bytes 262176 | tf_op jit(solution)/shard_map/ppermute | solution.py:48
  56.3 0.5 collective-permute-start.19
  56.8 0.7 copy-done.5
  57.5 1.0 picked_rows.1
  58.5 1.4 collective-permute-start
  59.9 2.4 %collective-permute-start.1 = (bf16[128,896]{1,0:T(8,128)(2,1)S(1)}, bf16[128,896]{1,0:T(8,128)(2,1)S(1)}, u32[]{:S(2)}, u32[]{:S(2)}) collective-permute-start(bf16[128,896]{1,0:T(8,128)(2,1)S(1)} %bitcast.27), channel_id=1, source_target_pairs={{0,4},{1,5},{2,6},{3,7},{4,0},{5,1},{6,2},{7,3},{8,12},{9,13},{10,... | collective-permute-start | bytes 688136 | tf_op jit(solution)/shard_map/ppermute | solution.py:48
  62.3 1.6 collective-permute-start.2
  63.9 0.5 collective-permute-start.3
  64.4 4.4 %collective-permute-done.r_1_ = bf16[128,896]{1,0:T(8,128)(2,1)S(1)} collective-permute-done((bf16[128,896]{1,0:T(8,128)(2,1)S(1)}, bf16[128,896]{1,0:T(8,128)(2,1)S(1)}, u32[]{:S(2)}, u32[]{:S(2)}) %collective-permute-start) | collective-permute-done | bytes 229408 | tf_op jit(solution)/shard_map/ppermute | solution.py:48
  68.8 3.9 %collective-permute-done.1.r_2_ = bf16[128,896]{1,0:T(8,128)(2,1)S(1)} collective-permute-done((bf16[128,896]{1,0:T(8,128)(2,1)S(1)}, bf16[128,896]{1,0:T(8,128)(2,1)S(1)}, u32[]{:S(2)}, u32[]{:S(2)}) %collective-permute-start.1) | collective-permute-done | bytes 229408 | tf_op jit(solution)/shard_map/ppermute | solution.py:48
  72.7 0.7 collective-permute-done.2.r_3_
  73.6 0.9 copy-done.6
  74.5 4.4 %d_attended.1.r_9_ = bf16[256,512]{1,0:T(8,128)(2,1)S(1)} custom-call(s32[8]{0:T(128)S(1)} %pad_add_fusion.r_0_, bf16[256,512]{1,0:T(8,128)(2,1)S(1)} %copy-done.4, bf16[256,512]{1,0:T(8,128)(2,1)S(1)} %collective-permute-done.14.r_2_, bf16[256,512]{1,0:T(8,128)(2,1)S(1)} %collective-permute-done.15.r_3_, bf16[256,512]{1,0:T(8,128)(2,1)S(1)} %collective-permute-done.16.r_4_, ...), custom_call_target="tpu_custom_call" | custom-call | tf_op jit(solution)/shard_map/d_attended/pallas_call | solution.py:140
  78.9 4.5 %queries.1.r_8_ = bf16[256,512]{1,0:T(8,128)(2,1)S(1)} custom-call(s32[8]{0:T(128)S(1)} %pad_add_fusion.r_0_, bf16[256,512]{1,0:T(8,128)(2,1)S(1)} %copy-done, bf16[256,512]{1,0:T(8,128)(2,1)S(1)} %collective-permute-done.7.r_2_, bf16[256,512]{1,0:T(8,128)(2,1)S(1)} %collective-permute-done.8.r_3_, bf16[256,512]{1,0:T(8,128)(2,1)S(1)} %collective-permute-done.9.r_4_, ...), custom_call_target="tpu_custom_call" | custom-call | tf_op jit(solution)/shard_map/queries/pallas_call | solution.py:108
  83.5 12.7 %attention.1 = (bf16[4,128,896]{2,1,0:T(8,128)(2,1)S(1)}, bf16[4,128,896]{2,1,0:T(8,128)(2,1)S(1)}, bf16[256,512]{1,0:T(8,128)(2,1)S(1)}) custom-call(bf16[128,896]{1,0:T(8,128)(2,1)S(1)} %bitcast.30, bf16[128,896]{1,0:T(8,128)(2,1)S(1)} %collective-permute-done.r_1_, bf16[128,896]{1,0:T(8,128)(2,1)S(1)} %collective-permute-done.1.r_2_, ...), custom_call_target="tpu_custom_call" | custom-call | tf_op jit(solution)/shard_map/attention/pallas_call | solution.py:239
  96.2 0.8 collective-permute-start.29
  97.0 4.1 %branches.1 = (bf16[4,256,512]{2,1,0:T(8,128)(2,1)S(1)}, bf16[4,256,512]{2,1,0:T(8,128)(2,1)S(1)}) custom-call(s32[8]{0:T(128)S(1)} %pad_add_fusion.r_0_, bf16[256,512]{1,0:T(8,128)(2,1)S(1)} %get-tuple-element.8.r_1_, bf16[512,4096]{1,0:T(8,128)(2,1)} %r_2_.1), custom_call_target="tpu_custom_call" | custom-call | tf_op jit(solution)/shard_map/branches/pallas_call | solution.py:175
  101.1 0.1 collective-permute-start.21
  101.2 0.2 add_convert_fusion.1
  101.5 2.2 %collective-permute-start.31 = (bf16[128,896]{1,0:T(8,128)(2,1)S(1)}, bf16[128,896]{1,0:T(8,128)(2,1)S(1)}, u32[]{:S(2)}, u32[]{:S(2)}) collective-permute-start(bf16[128,896]{1,0:T(8,128)(2,1)S(1)} %get-tuple-element.21), channel_id=1, source_target_pairs={{0,4},{1,5},{2,6},{3,7},{4,0},{5,1},{6,2},{7,3},{8,12},{9,13},{10,... | collective-permute-start | bytes 688136 | tf_op jit(solution)/shard_map/ppermute | solution.py:398
  103.8 1.3 collective-permute-start.32
  105.1 1.9 %collective-permute-start.30 = (bf16[128,896]{1,0:T(8,128)(2,1)S(1)}, bf16[128,896]{1,0:T(8,128)(2,1)S(1)}, u32[]{:S(2)}, u32[]{:S(2)}) collective-permute-start(bf16[128,896]{1,0:T(8,128)(2,1)S(1)} %get-tuple-element.22), channel_id=1, source_target_pairs={{0,6},{1,7},{2,0},{3,1},{4,2},{5,3},{6,4},{7,5},{8,14},{9,15},{10,... | collective-permute-start | bytes 688136 | tf_op jit(solution)/shard_map/ppermute | solution.py:398
  107.0 4.6 %collective-permute-done.31 = bf16[128,896]{1,0:T(8,128)(2,1)S(1)} collective-permute-done((bf16[128,896]{1,0:T(8,128)(2,1)S(1)}, bf16[128,896]{1,0:T(8,128)(2,1)S(1)}, u32[]{:S(2)}, u32[]{:S(2)}) %collective-permute-start.31) | collective-permute-done | bytes 229408 | tf_op jit(solution)/shard_map/ppermute | solution.py:398
  111.6 4.5 %collective-permute-done.32 = bf16[128,896]{1,0:T(8,128)(2,1)S(1)} collective-permute-done((bf16[128,896]{1,0:T(8,128)(2,1)S(1)}, bf16[128,896]{1,0:T(8,128)(2,1)S(1)}, u32[]{:S(2)}, u32[]{:S(2)}) %collective-permute-start.32) | collective-permute-done | bytes 229408 | tf_op jit(solution)/shard_map/ppermute | solution.py:398
  116.0 1.7 %placed_grads.1 = bf16[32,16,896]{2,1,0:T(8,128)(2,1)} custom-call(s32[32]{0:T(128)S(1)} %get-tuple-element.13.reading, bf16[8,16,896]{2,1,0:T(8,128)(2,1)S(1)} %bitcast.25, bf16[8,16,896]{2,1,0:T(8,128)(2,1)S(1)} %bitcast.33, bf16[8,16,896]{2,1,0:T(8,128)(2,1)S(1)} %bitcast.31, bf16[8,16,896]{2,1,0:T(8,128)(2,1)S(1)} %bitcast.32), custom_call_target="tpu_custom_call" | custom-call | tf_op jit(solution)/shard_map/placed_grads/pallas_call | solution.py:306
  117.8 9.9 %all-to-all-start.2 = ((bf16[32,16,896]{2,1,0:T(8,128)(2,1)}), bf16[32,16,896]{2,1,0:T(8,128)(2,1)S(1)}, u32[]{:S(2)}, u32[]{:S(2)}) async-start(bf16[32,16,896]{2,1,0:T(8,128)(2,1)} %placed_grads.1), calls=%async_computation.2 | async-start | bytes 1835008 | tf_op jit(solution)/shard_map/all_to_all | solution.py:403
  127.7 1.5 add_convert_fusion
  129.3 2.7 %collective-permute-start.22 = (bf16[256,512]{1,0:T(8,128)(2,1)S(1)}, bf16[256,512]{1,0:T(8,128)(2,1)S(1)}, u32[]{:S(2)}, u32[]{:S(2)}) collective-permute-start(bf16[256,512]{1,0:T(8,128)(2,1)S(1)} %get-tuple-element.17), channel_id=1, source_target_pairs={{0,6},{1,7},{2,0},{3,1},{4,2},{5,3},{6,4},{7,5},{8,14},{9,15},{10,... | collective-permute-start | bytes 786440 | tf_op jit(solution)/shard_map/ppermute | solution.py:57
  131.9 1.0 collective-permute-start.23
  132.9 9.9 %collective-permute-done.22 = bf16[256,512]{1,0:T(8,128)(2,1)S(1)} collective-permute-done((bf16[256,512]{1,0:T(8,128)(2,1)S(1)}, bf16[256,512]{1,0:T(8,128)(2,1)S(1)}, u32[]{:S(2)}, u32[]{:S(2)}) %collective-permute-start.22) | collective-permute-done | bytes 262176 | tf_op jit(solution)/shard_map/ppermute | solution.py:57
  142.8 3.7 %collective-permute-done.24 = bf16[256,512]{1,0:T(8,128)(2,1)S(1)} collective-permute-done((bf16[256,512]{1,0:T(8,128)(2,1)S(1)}, bf16[256,512]{1,0:T(8,128)(2,1)S(1)}, u32[]{:S(2)}, u32[]{:S(2)}) %collective-permute-start.24) | collective-permute-done | bytes 262176 | tf_op jit(solution)/shard_map/ppermute | solution.py:57
  146.5 0.3 fusion
  146.7 0.1 collective-permute-start.25
  146.8 0.8 dynamic_slice.3
  147.6 0.4 collective-permute-done.25
  148.0 2.1 %collective-permute-start.27 = (f32[256]{0:T(256)S(1)}, f32[256]{0:T(256)S(1)}, u32[]{:S(2)}, u32[]{:S(2)}) collective-permute-start(f32[256]{0:T(256)S(1)} %add.86), channel_id=1, source_target_pairs={{0,4},{1,5},{2,6},{3,7},{4,0},{5,1},{6,2},{7,3},{8,12},{9,13},{10,... | collective-permute-start | bytes 3080 | tf_op jit(solution)/shard_map/ppermute | solution.py:413
  150.0 1.6 collective-permute-start.28
  151.6 0.1 select_reduce_fusion.1.slot
  151.7 1.0 collective-permute-done.26
  152.7 0.3 collective-permute-done.27
  153.0 0.6 collective-permute-done.28
  153.6 0.8 fusion.2
  154.5 1.9 %d_encodings.1 = bf16[8,16,896]{2,1,0:T(8,128)(2,1)} custom-call(s32[8]{0:T(128)S(1)} %select_reduce_fusion.1.slot, bf16[32,16,896]{2,1,0:T(8,128)(2,1)S(1)} %all-to-all-done.2.back, bf16[8,16,896]{2,1,0:T(8,128)(2,1)S(1)} %copy-done.3, f32[1,1,896]{2,1,0:T(1,128)S(1)} %reshape.103.gain), custom_call_target="tpu_custom_call" | custom-call | tf_op jit(solution)/shard_map/d_encodings/pallas_call | solution.py:334
  (55 shorter events, 0.4 us)
Async XLA Ops:
  0.6 30.2 %copy-start = (bf16[256,512]{1,0:T(8,128)(2,1)S(1)}, bf16[256,512]{1,0:T(8,128)(2,1)}, u32[]{:S(2)}) copy-start(bf16[256,512]{1,0:T(8,128)(2,1)} %r_1_.2) | copy-start | bytes 786436
  2.3 20.2 %all-to-all-start = ((s32[32,1,1]{2,1,0:T(1,128)}), s32[32,1,1]{2,1,0:T(1,128)S(1)}, u32[]{:S(2)}, u32[]{:S(2)}) async-start(s32[32,1,1]{2,1,0:T(1,128)} %copy.21), calls=%async_computation | async-start | bytes 32768 | tf_op jit(solution)/shard_map/all_to_all | solution.py:379
  23.2 0.9 copy-start.2
  24.1 12.5 %copy-start.4 = (bf16[256,512]{1,0:T(8,128)(2,1)S(1)}, bf16[256,512]{1,0:T(8,128)(2,1)}, u32[]{:S(2)}) copy-start(bf16[256,512]{1,0:T(8,128)(2,1)} %r_1_.3) | copy-start | bytes 786436
  24.1 49.3 %copy-start.8 = (f32[4096]{0:T(1024)S(1)}, f32[4096]{0:T(1024)}, u32[]{:S(2)}) copy-start(f32[4096]{0:T(1024)} %param.13) | copy-start | bytes 49156
  25.8 31.7 %all-to-all-start.1 = ((bf16[32,16,896]{2,1,0:T(8,128)(2,1)}), bf16[32,16,896]{2,1,0:T(8,128)(2,1)S(1)}, u32[]{:S(2)}, u32[]{:S(2)}) async-start(bf16[32,16,896]{2,1,0:T(8,128)(2,1)} %outgoing_rows.1), calls=%async_computation.1 | async-start | bytes 1835008 | tf_op jit(solution)/shard_map/all_to_all | solution.py:388
  30.8 9.6 %collective-permute-start.7 = (bf16[256,512]{1,0:T(8,128)(2,1)S(1)}, bf16[256,512]{1,0:T(8,128)(2,1)S(1)}, u32[]{:S(2)}, u32[]{:S(2)}) collective-permute-start(bf16[256,512]{1,0:T(8,128)(2,1)S(1)} %copy-done), channel_id=1, source_target_pairs={{0,2},{1,3},{2,4},{3,5},{4,6},{5,7},{6,0},{7,1},{8,10},{9,11},{10,... | collective-permute-start | bytes 786440 | tf_op jit(solution)/shard_map/ppermute | solution.py:48
  32.4 15.6 %collective-permute-start.8 = (bf16[256,512]{1,0:T(8,128)(2,1)S(1)}, bf16[256,512]{1,0:T(8,128)(2,1)S(1)}, u32[]{:S(2)}, u32[]{:S(2)}) collective-permute-start(bf16[256,512]{1,0:T(8,128)(2,1)S(1)} %copy-done), channel_id=1, source_target_pairs={{0,4},{1,5},{2,6},{3,7},{4,0},{5,1},{6,2},{7,3},{8,12},{9,13},{10,... | collective-permute-start | bytes 786440 | tf_op jit(solution)/shard_map/ppermute | solution.py:48
  35.1 13.4 %collective-permute-start.9 = (bf16[256,512]{1,0:T(8,128)(2,1)S(1)}, bf16[256,512]{1,0:T(8,128)(2,1)S(1)}, u32[]{:S(2)}, u32[]{:S(2)}) collective-permute-start(bf16[256,512]{1,0:T(8,128)(2,1)S(1)} %copy-done), channel_id=1, source_target_pairs={{0,6},{1,7},{2,0},{3,1},{4,2},{5,3},{6,4},{7,5},{8,14},{9,15},{10,... | collective-permute-start | bytes 786440 | tf_op jit(solution)/shard_map/ppermute | solution.py:48
  36.6 12.0 %collective-permute-start.10 = (bf16[256,512]{1,0:T(8,128)(2,1)S(1)}, bf16[256,512]{1,0:T(8,128)(2,1)S(1)}, u32[]{:S(2)}, u32[]{:S(2)}) collective-permute-start(bf16[256,512]{1,0:T(8,128)(2,1)S(1)} %copy-done), channel_id=1, source_target_pairs={{0,1},{1,0},{2,3},{3,2},{4,5},{5,4},{6,7},{7,6},{8,9},{9,8},{10,11... | collective-permute-start | bytes 786440 | tf_op jit(solution)/shard_map/ppermute | solution.py:49
  36.6 15.5 %collective-permute-start.14 = (bf16[256,512]{1,0:T(8,128)(2,1)S(1)}, bf16[256,512]{1,0:T(8,128)(2,1)S(1)}, u32[]{:S(2)}, u32[]{:S(2)}) collective-permute-start(bf16[256,512]{1,0:T(8,128)(2,1)S(1)} %copy-done.4), channel_id=1, source_target_pairs={{0,2},{1,3},{2,4},{3,5},{4,6},{5,7},{6,0},{7,1},{8,10},{9,11},{10,... | collective-permute-start | bytes 786440 | tf_op jit(solution)/shard_map/ppermute | solution.py:48
  40.5 15.8 %collective-permute-start.15 = (bf16[256,512]{1,0:T(8,128)(2,1)S(1)}, bf16[256,512]{1,0:T(8,128)(2,1)S(1)}, u32[]{:S(2)}, u32[]{:S(2)}) collective-permute-start(bf16[256,512]{1,0:T(8,128)(2,1)S(1)} %copy-done.4), channel_id=1, source_target_pairs={{0,4},{1,5},{2,6},{3,7},{4,0},{5,1},{6,2},{7,3},{8,12},{9,13},{10,... | collective-permute-start | bytes 786440 | tf_op jit(solution)/shard_map/ppermute | solution.py:48
  48.0 8.3 %collective-permute-start.16 = (bf16[256,512]{1,0:T(8,128)(2,1)S(1)}, bf16[256,512]{1,0:T(8,128)(2,1)S(1)}, u32[]{:S(2)}, u32[]{:S(2)}) collective-permute-start(bf16[256,512]{1,0:T(8,128)(2,1)S(1)} %copy-done.4), channel_id=1, source_target_pairs={{0,6},{1,7},{2,0},{3,1},{4,2},{5,3},{6,4},{7,5},{8,14},{9,15},{10,... | collective-permute-start | bytes 786440 | tf_op jit(solution)/shard_map/ppermute | solution.py:48
  48.6 8.2 %collective-permute-start.17 = (bf16[256,512]{1,0:T(8,128)(2,1)S(1)}, bf16[256,512]{1,0:T(8,128)(2,1)S(1)}, u32[]{:S(2)}, u32[]{:S(2)}) collective-permute-start(bf16[256,512]{1,0:T(8,128)(2,1)S(1)} %copy-done.4), channel_id=1, source_target_pairs={{0,1},{1,0},{2,3},{3,2},{4,5},{5,4},{6,7},{7,6},{8,9},{9,8},{10,11... | collective-permute-start | bytes 786440 | tf_op jit(solution)/shard_map/ppermute | solution.py:49
  48.6 9.9 %collective-permute-start.11 = (bf16[256,512]{1,0:T(8,128)(2,1)S(1)}, bf16[256,512]{1,0:T(8,128)(2,1)}, u32[]{:S(2)}, u32[]{:S(2)}) collective-permute-start(bf16[256,512]{1,0:T(8,128)(2,1)S(1)} %collective-permute-done.7.r_2_), channel_id=1, source_target_pairs={{0,1},{1,0},{2,3},{3,2},{4,5},{5,4},{6,7},{7,6},{8,9},{9,8},{10,11... | collective-permute-start | bytes 786440 | tf_op jit(solution)/shard_map/ppermute | solution.py:49
  52.1 7.8 %collective-permute-start.12 = (bf16[256,512]{1,0:T(8,128)(2,1)S(1)}, bf16[256,512]{1,0:T(8,128)(2,1)}, u32[]{:S(2)}, u32[]{:S(2)}) collective-permute-start(bf16[256,512]{1,0:T(8,128)(2,1)S(1)} %collective-permute-done.8.r_3_), channel_id=1, source_target_pairs={{0,1},{1,0},{2,3},{3,2},{4,5},{5,4},{6,7},{7,6},{8,9},{9,8},{10,11... | collective-permute-start | bytes 786440 | tf_op jit(solution)/shard_map/ppermute | solution.py:49
  56.3 6.0 %collective-permute-start.18 = (bf16[256,512]{1,0:T(8,128)(2,1)S(1)}, bf16[256,512]{1,0:T(8,128)(2,1)}, u32[]{:S(2)}, u32[]{:S(2)}) collective-permute-start(bf16[256,512]{1,0:T(8,128)(2,1)S(1)} %collective-permute-done.14.r_2_), channel_id=1, source_target_pairs={{0,1},{1,0},{2,3},{3,2},{4,5},{5,4},{6,7},{7,6},{8,9},{9,8},{10,11... | collective-permute-start | bytes 786440 | tf_op jit(solution)/shard_map/ppermute | solution.py:49
  56.3 7.6 %collective-permute-start.19 = (bf16[256,512]{1,0:T(8,128)(2,1)S(1)}, bf16[256,512]{1,0:T(8,128)(2,1)}, u32[]{:S(2)}, u32[]{:S(2)}) collective-permute-start(bf16[256,512]{1,0:T(8,128)(2,1)S(1)} %collective-permute-done.15.r_3_), channel_id=1, source_target_pairs={{0,1},{1,0},{2,3},{3,2},{4,5},{5,4},{6,7},{7,6},{8,9},{9,8},{10,11... | collective-permute-start | bytes 786440 | tf_op jit(solution)/shard_map/ppermute | solution.py:49
  56.8 0.7 copy-start.5
  57.5 6.4 %collective-permute-start.20 = (bf16[256,512]{1,0:T(8,128)(2,1)S(1)}, bf16[256,512]{1,0:T(8,128)(2,1)}, u32[]{:S(2)}, u32[]{:S(2)}) collective-permute-start(bf16[256,512]{1,0:T(8,128)(2,1)S(1)} %collective-permute-done.16.r_4_), channel_id=1, source_target_pairs={{0,1},{1,0},{2,3},{3,2},{4,5},{5,4},{6,7},{7,6},{8,9},{9,8},{10,11... | collective-permute-start | bytes 786440 | tf_op jit(solution)/shard_map/ppermute | solution.py:49
  58.5 10.3 %collective-permute-start = (bf16[128,896]{1,0:T(8,128)(2,1)S(1)}, bf16[128,896]{1,0:T(8,128)(2,1)S(1)}, u32[]{:S(2)}, u32[]{:S(2)}) collective-permute-start(bf16[128,896]{1,0:T(8,128)(2,1)S(1)} %bitcast.26), channel_id=1, source_target_pairs={{0,2},{1,3},{2,4},{3,5},{4,6},{5,7},{6,0},{7,1},{8,10},{9,11},{10,... | collective-permute-start | bytes 688136 | tf_op jit(solution)/shard_map/ppermute | solution.py:48
  59.9 12.8 %collective-permute-start.1 = (bf16[128,896]{1,0:T(8,128)(2,1)S(1)}, bf16[128,896]{1,0:T(8,128)(2,1)S(1)}, u32[]{:S(2)}, u32[]{:S(2)}) collective-permute-start(bf16[128,896]{1,0:T(8,128)(2,1)S(1)} %bitcast.27), channel_id=1, source_target_pairs={{0,4},{1,5},{2,6},{3,7},{4,0},{5,1},{6,2},{7,3},{8,12},{9,13},{10,... | collective-permute-start | bytes 688136 | tf_op jit(solution)/shard_map/ppermute | solution.py:48
  62.3 11.1 %collective-permute-start.2 = (bf16[128,896]{1,0:T(8,128)(2,1)S(1)}, bf16[128,896]{1,0:T(8,128)(2,1)}, u32[]{:S(2)}, u32[]{:S(2)}) collective-permute-start(bf16[128,896]{1,0:T(8,128)(2,1)S(1)} %bitcast.28), channel_id=1, source_target_pairs={{0,6},{1,7},{2,0},{3,1},{4,2},{5,3},{6,4},{7,5},{8,14},{9,15},{10,... | collective-permute-start | bytes 688136 | tf_op jit(solution)/shard_map/ppermute | solution.py:48
  63.9 15.0 %collective-permute-start.13 = (bf16[256,512]{1,0:T(8,128)(2,1)S(1)}, bf16[256,512]{1,0:T(8,128)(2,1)S(1)}, u32[]{:S(2)}, u32[]{:S(2)}) collective-permute-start(bf16[256,512]{1,0:T(8,128)(2,1)S(1)} %collective-permute-done.9.r_4_), channel_id=1, source_target_pairs={{0,1},{1,0},{2,3},{3,2},{4,5},{5,4},{6,7},{7,6},{8,9},{9,8},{10,11... | collective-permute-start | bytes 786440 | tf_op jit(solution)/shard_map/ppermute | solution.py:49
  63.9 19.5 %collective-permute-start.3 = (bf16[128,896]{1,0:T(8,128)(2,1)S(1)}, bf16[128,896]{1,0:T(8,128)(2,1)}, u32[]{:S(2)}, u32[]{:S(2)}) collective-permute-start(bf16[128,896]{1,0:T(8,128)(2,1)S(1)} %bitcast.29), channel_id=1, source_target_pairs={{0,1},{1,0},{2,3},{3,2},{4,5},{5,4},{6,7},{7,6},{8,9},{9,8},{10,11... | collective-permute-start | bytes 688136 | tf_op jit(solution)/shard_map/ppermute | solution.py:49
  68.8 14.7 %collective-permute-start.4 = (bf16[128,896]{1,0:T(8,128)(2,1)S(1)}, bf16[128,896]{1,0:T(8,128)(2,1)}, u32[]{:S(2)}, u32[]{:S(2)}) collective-permute-start(bf16[128,896]{1,0:T(8,128)(2,1)S(1)} %collective-permute-done.r_1_), channel_id=1, source_target_pairs={{0,1},{1,0},{2,3},{3,2},{4,5},{5,4},{6,7},{7,6},{8,9},{9,8},{10,11... | collective-permute-start | bytes 688136 | tf_op jit(solution)/shard_map/ppermute | solution.py:49
  72.7 10.7 %collective-permute-start.5 = (bf16[128,896]{1,0:T(8,128)(2,1)S(1)}, bf16[128,896]{1,0:T(8,128)(2,1)}, u32[]{:S(2)}, u32[]{:S(2)}) collective-permute-start(bf16[128,896]{1,0:T(8,128)(2,1)S(1)} %collective-permute-done.1.r_2_), channel_id=1, source_target_pairs={{0,1},{1,0},{2,3},{3,2},{4,5},{5,4},{6,7},{7,6},{8,9},{9,8},{10,11... | collective-permute-start | bytes 688136 | tf_op jit(solution)/shard_map/ppermute | solution.py:49
  73.4 10.0 %collective-permute-start.6 = (bf16[128,896]{1,0:T(8,128)(2,1)}, bf16[128,896]{1,0:T(8,128)(2,1)}, u32[]{:S(2)}, u32[]{:S(2)}) collective-permute-start(bf16[128,896]{1,0:T(8,128)(2,1)} %collective-permute-done.2.r_3_), channel_id=1, source_target_pairs={{0,1},{1,0},{2,3},{3,2},{4,5},{5,4},{6,7},{7,6},{8,9},{9,8},{10,11... | collective-permute-start | bytes 688136 | tf_op jit(solution)/shard_map/ppermute | solution.py:49
  73.5 1.0 copy-start.6
  78.9 4.6 %copy-start.1 = (bf16[896,512]{1,0:T(8,128)(2,1)S(1)}, bf16[896,512]{1,0:T(8,128)(2,1)}, u32[]{:S(2)}) copy-start(bf16[896,512]{1,0:T(8,128)(2,1)} %r_10_.3) | copy-start | bytes 2752516
  96.2 5.0 %collective-permute-start.29 = (bf16[4,128,896]{2,1,0:T(8,128)(2,1)S(1)}, bf16[4,128,896]{2,1,0:T(8,128)(2,1)S(1)}, u32[]{:S(2)}, u32[]{:S(2)}) collective-permute-start(bf16[4,128,896]{2,1,0:T(8,128)(2,1)S(1)} %get-tuple-element.12), channel_id=1, source_target_pairs={{0,1},{1,0},{2,3},{3,2},{4,5},{5,4},{6,7},{7,6},{8,9},{9,8},{10,11... | collective-permute-start | bytes 2752520 | tf_op jit(solution)/shard_map/ppermute | solution.py:395
  101.1 26.6 %collective-permute-start.21 = (bf16[4,256,512]{2,1,0:T(8,128)(2,1)S(1)}, bf16[4,256,512]{2,1,0:T(8,128)(2,1)}, u32[]{:S(2)}, u32[]{:S(2)}) collective-permute-start(bf16[4,256,512]{2,1,0:T(8,128)(2,1)S(1)} %get-tuple-element.10), channel_id=1, source_target_pairs={{0,1},{1,0},{2,3},{3,2},{4,5},{5,4},{6,7},{7,6},{8,9},{9,8},{10,11... | collective-permute-start | bytes 3145736 | tf_op jit(solution)/shard_map/ppermute | solution.py:53
  101.5 10.0 %collective-permute-start.31 = (bf16[128,896]{1,0:T(8,128)(2,1)S(1)}, bf16[128,896]{1,0:T(8,128)(2,1)S(1)}, u32[]{:S(2)}, u32[]{:S(2)}) collective-permute-start(bf16[128,896]{1,0:T(8,128)(2,1)S(1)} %get-tuple-element.21), channel_id=1, source_target_pairs={{0,4},{1,5},{2,6},{3,7},{4,0},{5,1},{6,2},{7,3},{8,12},{9,13},{10,... | collective-permute-start | bytes 688136 | tf_op jit(solution)/shard_map/ppermute | solution.py:398
  103.8 12.3 %collective-permute-start.32 = (bf16[128,896]{1,0:T(8,128)(2,1)S(1)}, bf16[128,896]{1,0:T(8,128)(2,1)S(1)}, u32[]{:S(2)}, u32[]{:S(2)}) collective-permute-start(bf16[128,896]{1,0:T(8,128)(2,1)S(1)} %get-tuple-element.20), channel_id=1, source_target_pairs={{0,2},{1,3},{2,4},{3,5},{4,6},{5,7},{6,0},{7,1},{8,10},{9,11},{10,... | collective-permute-start | bytes 688136 | tf_op jit(solution)/shard_map/ppermute | solution.py:398
  105.1 10.9 %collective-permute-start.30 = (bf16[128,896]{1,0:T(8,128)(2,1)S(1)}, bf16[128,896]{1,0:T(8,128)(2,1)S(1)}, u32[]{:S(2)}, u32[]{:S(2)}) collective-permute-start(bf16[128,896]{1,0:T(8,128)(2,1)S(1)} %get-tuple-element.22), channel_id=1, source_target_pairs={{0,6},{1,7},{2,0},{3,1},{4,2},{5,3},{6,4},{7,5},{8,14},{9,15},{10,... | collective-permute-start | bytes 688136 | tf_op jit(solution)/shard_map/ppermute | solution.py:398
  117.8 36.7 %all-to-all-start.2 = ((bf16[32,16,896]{2,1,0:T(8,128)(2,1)}), bf16[32,16,896]{2,1,0:T(8,128)(2,1)S(1)}, u32[]{:S(2)}, u32[]{:S(2)}) async-start(bf16[32,16,896]{2,1,0:T(8,128)(2,1)} %placed_grads.1), calls=%async_computation.2 | async-start | bytes 1835008 | tf_op jit(solution)/shard_map/all_to_all | solution.py:403
  129.2 25.3 %copy-start.3 = (bf16[8,16,896]{2,1,0:T(8,128)(2,1)S(1)}, bf16[8,16,896]{2,1,0:T(8,128)(2,1)}, u32[]{:S(2)}) copy-start(bf16[8,16,896]{2,1,0:T(8,128)(2,1)} %enc.3) | copy-start | bytes 688132
  129.3 13.5 %collective-permute-start.22 = (bf16[256,512]{1,0:T(8,128)(2,1)S(1)}, bf16[256,512]{1,0:T(8,128)(2,1)S(1)}, u32[]{:S(2)}, u32[]{:S(2)}) collective-permute-start(bf16[256,512]{1,0:T(8,128)(2,1)S(1)} %get-tuple-element.17), channel_id=1, source_target_pairs={{0,6},{1,7},{2,0},{3,1},{4,2},{5,3},{6,4},{7,5},{8,14},{9,15},{10,... | collective-permute-start | bytes 786440 | tf_op jit(solution)/shard_map/ppermute | solution.py:57
  131.9 10.8 %collective-permute-start.23 = (bf16[256,512]{1,0:T(8,128)(2,1)S(1)}, bf16[256,512]{1,0:T(8,128)(2,1)S(1)}, u32[]{:S(2)}, u32[]{:S(2)}) collective-permute-start(bf16[256,512]{1,0:T(8,128)(2,1)S(1)} %get-tuple-element.19), channel_id=1, source_target_pairs={{0,4},{1,5},{2,6},{3,7},{4,0},{5,1},{6,2},{7,3},{8,12},{9,13},{10,... | collective-permute-start | bytes 786440 | tf_op jit(solution)/shard_map/ppermute | solution.py:57
  132.9 13.5 %collective-permute-start.24 = (bf16[256,512]{1,0:T(8,128)(2,1)S(1)}, bf16[256,512]{1,0:T(8,128)(2,1)S(1)}, u32[]{:S(2)}, u32[]{:S(2)}) collective-permute-start(bf16[256,512]{1,0:T(8,128)(2,1)S(1)} %get-tuple-element.18), channel_id=1, source_target_pairs={{0,2},{1,3},{2,4},{3,5},{4,6},{5,7},{6,0},{7,1},{8,10},{9,11},{10,... | collective-permute-start | bytes 786440 | tf_op jit(solution)/shard_map/ppermute | solution.py:57
  146.7 9.7 %copy-start.7 = (bf16[256,512]{1,0:T(8,128)(2,1)}, bf16[256,512]{1,0:T(8,128)(2,1)S(1)}, u32[]{:S(2)}) copy-start(bf16[256,512]{1,0:T(8,128)(2,1)S(1)} %get-tuple-element.16) | copy-start | bytes 786436
  146.7 1.2 collective-permute-start.25
  148.0 4.8 %collective-permute-start.26 = (f32[256]{0:T(256)S(1)}, f32[256]{0:T(256)S(1)}, u32[]{:S(2)}, u32[]{:S(2)}) collective-permute-start(f32[256]{0:T(256)S(1)} %add.86), channel_id=1, source_target_pairs={{0,2},{1,3},{2,4},{3,5},{4,6},{5,7},{6,0},{7,1},{8,10},{9,11},{10,... | collective-permute-start | bytes 3080 | tf_op jit(solution)/shard_map/ppermute | solution.py:413
  148.0 5.1 %collective-permute-start.27 = (f32[256]{0:T(256)S(1)}, f32[256]{0:T(256)S(1)}, u32[]{:S(2)}, u32[]{:S(2)}) collective-permute-start(f32[256]{0:T(256)S(1)} %add.86), channel_id=1, source_target_pairs={{0,4},{1,5},{2,6},{3,7},{4,0},{5,1},{6,2},{7,3},{8,12},{9,13},{10,... | collective-permute-start | bytes 3080 | tf_op jit(solution)/shard_map/ppermute | solution.py:413
  150.0 3.6 %collective-permute-start.28 = (f32[256]{0:T(256)S(1)}, f32[256]{0:T(256)S(1)}, u32[]{:S(2)}, u32[]{:S(2)}) collective-permute-start(f32[256]{0:T(256)S(1)} %add.86), channel_id=1, source_target_pairs={{0,6},{1,7},{2,0},{3,1},{4,2},{5,3},{6,4},{7,5},{8,14},{9,15},{10,... | collective-permute-start | bytes 3080 | tf_op jit(solution)/shard_map/ppermute | solution.py:413
